TPU v7x, 256 devices: a whole 4x4x8 slice. The times are simulated.
256 devices in a mesh: gx: 8 (over x, core), gy: 8 (over z_lo, y), gz: 4 (over z_hi).
Axes of the slice: x: 4, y: 4, z: 8 (z_hi: 4, z_lo: 2; z = z_hi * 2 + z_lo), core: 2. Of those that a mesh axis runs over, the one named last changes fastest.
Arguments:
- bead_pos: float32 [3, 16, 32, 8, 128], P(None, 'gx', 'gy', 'gz'), may hold values from 0 to 3
- bead_vel: float32 [3, 16, 32, 8, 128], P(None, 'gx', 'gy', 'gz'), may hold values from -6 to 6
- bead_force: float32 [3, 16, 32, 8, 128], P(None, 'gx', 'gy', 'gz'), may hold values from -60 to 60
- cell_count: int32 [16, 32, 8], P('gx', 'gy', 'gz'), may hold values from 0 to 128
- pair_seed: int32 [16, 32, 8, 128], P('gx', 'gy', 'gz'), may hold values from 0 to 4095
- bead_half: int32 [16, 32, 8, 128], P('gx', 'gy', 'gz'), may hold values from 0 to 1
- grid_vel: float32 [3, 16, 32, 16], P(None, 'gx', ('gy', 'gz')), may hold values from -6 to 6
- correlation_map: int32 [16, 32, 16], P('gx', ('gy', 'gz')), may hold values 0 or 1
Outputs:
- new_positions: float32 [3, 16, 32, 8, 128], P(None, 'gx', 'gy', 'gz')
- new_velocities: float32 [3, 16, 32, 8, 128], P(None, 'gx', 'gy', 'gz')
- grid_velocity: float32 [3, 16, 32, 16], P(None, 'gx', ('gy', 'gz'))
- pressure: float32 [16, 32, 16], P('gx', ('gy', 'gz'))
- brick_velocity: float32 [3, 16, 32, 16], P(None, 'gx', 'gy', 'gz')
Inputs may be any that keep to these rules, and one draw needn't show every extreme that they name: `cell_count`: slots below a cell's count hold beads, the others are padding.
All inputs are finite; a program needn't handle non-finite values. No bound on the sum of `correlation_map` on one device may be relied on, other than what follows from the above.
Results may differ from a plain program's by a relative error of at most 0.0003.
Values sent between devices are 32-bit elements; how exact they have to be, the bound alone decides.
No kernel may reach another device: no remote copies, remote signals or barrier semaphores. Data moves between devices by JAX's collectives and lax.ppermute only.
A program may use at most 64 MiB of HBM per device.

v0:
```python
import math

import jax
import jax.numpy as jnp
import numpy as np
from jax import lax
from jax.sharding import PartitionSpec as P

STEPS = 2
ITERS = 4


cell_edge = 3.0
conserve = 25.0
friction = 4.5
noise_scale = 3.0 * math.sqrt(12.0) / math.sqrt(0.04)
time_step = 0.04
predict_weight = 0.65
couple_rate = 0.5
hash_prime = 4093


def with_halo(block, sides, width, periodic):
    for axis, dim in sides:
        count = lax.axis_size(axis)
        forward = [(i, i + 1) for i in range(count - 1)]
        if periodic:
            forward.append((count - 1, 0))
        backward = [(target, source) for source, target in forward]
        low = lax.ppermute(
            lax.slice_in_dim(block, block.shape[dim] - width, None, axis=dim), axis, forward
        )
        high = lax.ppermute(lax.slice_in_dim(block, 0, width, axis=dim), axis, backward)
        block = jnp.concatenate([low, block, high], axis=dim)
    return block


def pair_sum(center, padded, step_tag):
    extent_x, extent_y, extent_z = (center.shape[1], center.shape[2], center.shape[3])
    slot_count = center.shape[4]
    seed_own = center[6].astype(jnp.int32)[..., :, None]
    offsets_y = np.repeat(np.array([oy for oy in (-1, 0, 1) for oz in (-1, 0, 1)]), slot_count)
    offsets_z = np.repeat(np.array([oz for oy in (-1, 0, 1) for oz in (-1, 0, 1)]), slot_count)
    shift_y = jnp.asarray(offsets_y * cell_edge, dtype=jnp.float32)
    shift_z = jnp.asarray(offsets_z * cell_edge, dtype=jnp.float32)
    totals = [jnp.zeros(center.shape[1:], jnp.float32) for axis_k in range(3)]
    for offset_x in (-1, 0, 1):
        pieces = []
        for offset_y in (-1, 0, 1):
            for offset_z in (-1, 0, 1):
                pieces.append(
                    padded[
                        :,
                        1 + offset_x : 1 + offset_x + extent_x,
                        1 + offset_y : 1 + offset_y + extent_y,
                        1 + offset_z : 1 + offset_z + extent_z,
                        :,
                    ]
                )
        nearby = jnp.concatenate(pieces, axis=-1)
        shifts = (cell_edge * offset_x, shift_y, shift_z)
        deltas = [
            center[axis_k][..., :, None] - nearby[axis_k][..., None, :] - shifts[axis_k]
            for axis_k in range(3)
        ]
        square = deltas[0] * deltas[0] + deltas[1] * deltas[1] + deltas[2] * deltas[2]
        weight = jnp.maximum(1.0 - square, 0.0) * nearby[7][..., None, :]
        closing = deltas[0] * (center[3][..., :, None] - nearby[3][..., None, :])
        closing = closing + deltas[1] * (center[4][..., :, None] - nearby[4][..., None, :])
        closing = closing + deltas[2] * (center[5][..., :, None] - nearby[5][..., None, :])
        seed_other = nearby[6].astype(jnp.int32)[..., None, :]
        hashed = jnp.remainder(
            seed_own * seed_other + (seed_own + seed_other) * step_tag, hash_prime
        )
        random_term = (hashed.astype(jnp.float32) / hash_prime - 0.5) * noise_scale
        strength = weight * (conserve + random_term) - friction * weight * weight * closing
        for axis_k in range(3):
            totals[axis_k] = totals[axis_k] + jnp.sum(strength * deltas[axis_k], axis=-1)
    return jnp.stack(totals) * center[7]


def bin_sums(velocity, occupied, bead_half):
    pieces = []
    for side_index in (0, 1):
        select = occupied * (bead_half == side_index).astype(jnp.float32)
        moments = jnp.sum(velocity * select[None], axis=-1)
        counted = jnp.sum(select, axis=-1)
        pieces.append(jnp.concatenate([moments, counted[None]], axis=0))
    joined = jnp.stack(pieces, axis=-1)
    extent = joined.shape
    return joined.reshape(extent[0], extent[1], extent[2], extent[3] * 2)


def couple(bin_totals, grid_field, coupled_flag):
    bin_mean = bin_totals[:3] / jnp.maximum(bin_totals[3], 1.0)
    return grid_field + couple_rate * coupled_flag * (bin_mean - grid_field)


def project(coupled_vel, pad, reduce_all):
    padded = pad(coupled_vel)
    divergence = padded[0, 2:, 1:-1, 1:-1] - padded[0, :-2, 1:-1, 1:-1]
    divergence = divergence + padded[1, 1:-1, 2:, 1:-1] - padded[1, 1:-1, :-2, 1:-1]
    divergence = 0.5 * (divergence + padded[2, 1:-1, 1:-1, 2:] - padded[2, 1:-1, 1:-1, :-2])
    residual = -divergence
    direction = residual
    pressure = jnp.zeros_like(residual)
    norm_now = reduce_all(residual * residual)
    for repeat in range(ITERS):
        operate_beside_all = pad(direction[None])[0]
        beside = operate_beside_all[2:, 1:-1, 1:-1] + operate_beside_all[:-2, 1:-1, 1:-1]
        beside = beside + operate_beside_all[1:-1, 2:, 1:-1] + operate_beside_all[1:-1, :-2, 1:-1]
        beside = beside + operate_beside_all[1:-1, 1:-1, 2:] + operate_beside_all[1:-1, 1:-1, :-2]
        applied = 6.0 * direction - beside
        step_length = norm_now / reduce_all(direction * applied)
        pressure = pressure + step_length * direction
        residual = residual - step_length * applied
        norm_next = reduce_all(residual * residual)
        direction = residual + norm_next / norm_now * direction
        norm_now = norm_next
    beside_all = pad(pressure[None])[0]
    gradient = jnp.stack(
        [
            beside_all[2:, 1:-1, 1:-1] - beside_all[:-2, 1:-1, 1:-1],
            beside_all[1:-1, 2:, 1:-1] - beside_all[1:-1, :-2, 1:-1],
            beside_all[1:-1, 1:-1, 2:] - beside_all[1:-1, 1:-1, :-2],
        ]
    )
    return (coupled_vel - 0.5 * gradient, pressure)


def global_total(values):
    return lax.psum(jnp.sum(values), ("gx", "gy", "gz"))


def per_device(
    bead_pos, bead_vel, bead_force, cell_count, pair_seed, bead_half, grid_vel, correlation_map
):
    occupied = (lax.broadcasted_iota(jnp.int32, pair_seed.shape, 3) < cell_count[..., None]).astype(
        jnp.float32
    )
    static = jnp.stack([pair_seed.astype(jnp.float32), occupied])
    position, velocity, current = (bead_pos, bead_vel, bead_force)

    def gather_beads(stacked):
        along_x = with_halo(stacked, (("gx", 1),), 1, True)
        return with_halo(along_x, (("gy", 2), ("gz", 3)), 1, False)

    for step_number in range(STEPS):
        step_tag = step_number + 3
        position = position + time_step * velocity + 0.5 * time_step * time_step * current
        guessed = velocity + predict_weight * time_step * current
        padded = gather_beads(jnp.concatenate([position, guessed, static]))
        predicted = pair_sum(padded[:, 1:-1, 1:-1, 1:-1], padded, step_tag)
        corrected = velocity + 0.5 * time_step * (current + predicted)
        padded = gather_beads(jnp.concatenate([position, corrected, static]))
        iterated = pair_sum(padded[:, 1:-1, 1:-1, 1:-1], padded, step_tag)
        velocity = velocity + 0.5 * time_step * (current + iterated)
        current = iterated
    bin_totals = bin_sums(velocity, occupied, bead_half)
    coupled_flag = correlation_map.astype(jnp.float32)

    def pad_owner(field):
        along_x = with_halo(field, (("gx", 1),), 1, True)
        along_y = with_halo(along_x, ((("gy", "gz"), 2),), 1, False)
        return jnp.pad(along_y, ((0, 0), (0, 0), (0, 0), (1, 1)))

    arrived = lax.all_to_all(bin_totals, "gz", split_axis=2, concat_axis=3, tiled=True)
    coupled_vel = couple(arrived, grid_vel, coupled_flag)
    grid_velocity, pressure = project(coupled_vel, pad_owner, global_total)
    brick_velocity = lax.all_to_all(grid_velocity, "gz", split_axis=3, concat_axis=2, tiled=True)
    return (position, velocity, grid_velocity, pressure, brick_velocity)


def solution(mesh):
    placed = (
        P(None, "gx", "gy", "gz", None),
        P(None, "gx", "gy", "gz", None),
        P(None, "gx", "gy", "gz", None),
        P("gx", "gy", "gz"),
        P("gx", "gy", "gz", None),
        P("gx", "gy", "gz", None),
        P(None, "gx", ("gy", "gz"), None),
        P("gx", ("gy", "gz"), None),
    )
    return jax.shard_map(
        per_device,
        mesh=mesh,
        in_specs=placed,
        out_specs=(
            P(None, "gx", "gy", "gz", None),
            P(None, "gx", "gy", "gz", None),
            P(None, "gx", ("gy", "gz"), None),
            P("gx", ("gy", "gz"), None),
            P(None, "gx", "gy", "gz"),
        ),
        check_vma=False,
    )
```

profile of v0, /device:TPU:24, one launch (start us, length us, event | category | flops | bytes accessed | tf_op | source)
XLA Modules:
  0.0 1053.2 jit_solution(14121440175185437875)
XLA Ops:
  3.1 2.9 collective-permute-start.1
  7.7 3.5 collective-permute-start.2
  11.2 2.4 collective-permute-start.3
  13.7 5.5 collective-permute-done.3
  19.4 5.2 collective-permute-start.4
  26.8 5.9 collective-permute-done.5
  35.0 21.1 %fusion.103 = (f32[2,4,2,128]{3,2,1,0:T(2,128)S(1)}, f32[2,4,2,128]{3,2,1,0:T(2,128)S(1)}, f32[2,4,2,128]{3,2,1,0:T(2,128)S(1)}) fusion(f32[2,4,2,1152]{3,2,1,0:T(2,128)S(1)} %get-tuple-element.373, f32[2,4,2,128]{3,2,1,0:T(2,128)S(1)} %get-tuple-element.370, f32[2,4,2,1152]{3,2,1,0:T(2,128)S(1)} %get-tuple-element.379, ...), kind=kLoop, calls=%fused_computation.139 | loop fusion | flops 110880768 | bytes 680960 | tf_op jit(solution)/shard_map/reduce_sum | solution.py:78
  56.1 21.6 %multiply_reduce_fusion.31 = (f32[2,4,2,128]{3,2,1,0:T(2,128)S(1)}, f32[2,4,2,128]{3,2,1,0:T(2,128)S(1)}, f32[2,4,2,128]{3,2,1,0:T(2,128)S(1)}) fusion(f32[2,4,2,1152]{3,2,1,0:T(2,128)S(1)} %get-tuple-element.172, f32[2,4,2,128]{3,2,1,0:T(2,128)S(1)} %get-tuple-element.370, f32[2,4,2,1152]{3,2,1,0:T(2,128)S(1)} %get-tuple-element.166, ...), kind=kLoop, calls=%fused_computation.257 | loop fusion | flops 113240064 | bytes 680960 | tf_op jit(solution)/shard_map/reduce_sum | solution.py:78
  77.7 21.6 %multiply_reduce_fusion.30 = (f32[2,4,2,128]{3,2,1,0:T(2,128)S(1)}, f32[2,4,2,128]{3,2,1,0:T(2,128)S(1)}, f32[2,4,2,128]{3,2,1,0:T(2,128)S(1)}) fusion(f32[2,4,2,1152]{3,2,1,0:T(2,128)S(1)} %get-tuple-element.180, f32[2,4,2,128]{3,2,1,0:T(2,128)S(1)} %get-tuple-element.370, f32[2,4,2,1152]{3,2,1,0:T(2,128)S(1)} %get-tuple-element.174, ...), kind=kLoop, calls=%fused_computation.245 | loop fusion | flops 113240064 | bytes 680960 | tf_op jit(solution)/shard_map/reduce_sum | solution.py:78
  99.5 2.9 collective-permute-start.7
  104.1 2.7 collective-permute-start.8
  106.8 3.2 collective-permute-start.9
  110.0 4.7 collective-permute-done.9
  115.0 5.3 collective-permute-start.10
  122.5 5.2 collective-permute-done.11
  129.5 21.2 %fusion.111 = (f32[2,4,2,128]{3,2,1,0:T(2,128)S(1)}, f32[2,4,2,128]{3,2,1,0:T(2,128)S(1)}, f32[2,4,2,128]{3,2,1,0:T(2,128)S(1)}) fusion(f32[2,4,2,1152]{3,2,1,0:T(2,128)S(1)} %get-tuple-element.140, f32[2,4,2,128]{3,2,1,0:T(2,128)S(1)} %get-tuple-element.370, f32[2,4,2,1152]{3,2,1,0:T(2,128)S(1)} %get-tuple-element.134, ...), kind=kLoop, calls=%fused_computation.147 | loop fusion | flops 110880768 | bytes 680960 | tf_op jit(solution)/shard_map/reduce_sum | solution.py:78
  150.6 21.6 %multiply_reduce_fusion.23 = (f32[2,4,2,128]{3,2,1,0:T(2,128)S(1)}, f32[2,4,2,128]{3,2,1,0:T(2,128)S(1)}, f32[2,4,2,128]{3,2,1,0:T(2,128)S(1)}) fusion(f32[2,4,2,1152]{3,2,1,0:T(2,128)S(1)} %get-tuple-element.148, f32[2,4,2,128]{3,2,1,0:T(2,128)S(1)} %get-tuple-element.370, f32[2,4,2,1152]{3,2,1,0:T(2,128)S(1)} %get-tuple-element.142, ...), kind=kLoop, calls=%fused_computation.232 | loop fusion | flops 113240064 | bytes 680960 | tf_op jit(solution)/shard_map/reduce_sum | solution.py:78
  172.2 21.6 %multiply_reduce_fusion.22 = (f32[2,4,2,128]{3,2,1,0:T(2,128)S(1)}, f32[2,4,2,128]{3,2,1,0:T(2,128)S(1)}, f32[2,4,2,128]{3,2,1,0:T(2,128)S(1)}) fusion(f32[2,4,2,1152]{3,2,1,0:T(2,128)S(1)} %get-tuple-element.156, f32[2,4,2,128]{3,2,1,0:T(2,128)S(1)} %get-tuple-element.370, f32[2,4,2,1152]{3,2,1,0:T(2,128)S(1)} %get-tuple-element.150, ...), kind=kLoop, calls=%fused_computation.220 | loop fusion | flops 113240064 | bytes 680960 | tf_op jit(solution)/shard_map/reduce_sum | solution.py:78
  194.0 2.9 collective-permute-start.13
  198.7 2.5 collective-permute-start.14
  201.2 3.3 collective-permute-start.15
  204.5 4.5 collective-permute-done.15
  209.3 3.6 collective-permute-start.16
  215.1 5.2 collective-permute-done.17
  222.1 21.2 %fusion.119 = (f32[2,4,2,128]{3,2,1,0:T(2,128)S(1)}, f32[2,4,2,128]{3,2,1,0:T(2,128)S(1)}, f32[2,4,2,128]{3,2,1,0:T(2,128)S(1)}) fusion(f32[2,4,2,1152]{3,2,1,0:T(2,128)S(1)} %get-tuple-element.116, f32[2,4,2,128]{3,2,1,0:T(2,128)S(1)} %get-tuple-element.338, f32[2,4,2,1152]{3,2,1,0:T(2,128)S(1)} %get-tuple-element.110, ...), kind=kLoop, calls=%fused_computation.155 | loop fusion | flops 110880768 | bytes 680960 | tf_op jit(solution)/shard_map/reduce_sum | solution.py:78
  243.3 21.6 %multiply_reduce_fusion.15 = (f32[2,4,2,128]{3,2,1,0:T(2,128)S(1)}, f32[2,4,2,128]{3,2,1,0:T(2,128)S(1)}, f32[2,4,2,128]{3,2,1,0:T(2,128)S(1)}) fusion(f32[2,4,2,1152]{3,2,1,0:T(2,128)S(1)} %get-tuple-element.124, f32[2,4,2,128]{3,2,1,0:T(2,128)S(1)} %get-tuple-element.338, f32[2,4,2,1152]{3,2,1,0:T(2,128)S(1)} %get-tuple-element.118, ...), kind=kLoop, calls=%fused_computation.207 | loop fusion | flops 113240064 | bytes 680960 | tf_op jit(solution)/shard_map/reduce_sum | solution.py:78
  264.9 21.6 %multiply_reduce_fusion.14 = (f32[2,4,2,128]{3,2,1,0:T(2,128)S(1)}, f32[2,4,2,128]{3,2,1,0:T(2,128)S(1)}, f32[2,4,2,128]{3,2,1,0:T(2,128)S(1)}) fusion(f32[2,4,2,1152]{3,2,1,0:T(2,128)S(1)} %get-tuple-element.132, f32[2,4,2,128]{3,2,1,0:T(2,128)S(1)} %get-tuple-element.338, f32[2,4,2,1152]{3,2,1,0:T(2,128)S(1)} %get-tuple-element.126, ...), kind=kLoop, calls=%fused_computation.195 | loop fusion | flops 113240064 | bytes 680960 | tf_op jit(solution)/shard_map/reduce_sum | solution.py:78
  286.6 2.9 collective-permute-start.19
  291.3 2.2 collective-permute-start.20
  293.5 3.6 collective-permute-start.21
  297.2 4.3 collective-permute-done.21
  301.7 2.8 collective-permute-start.22
  306.7 5.2 collective-permute-done.23
  313.7 21.2 %fusion.127 = (f32[2,4,2,128]{3,2,1,0:T(2,128)S(1)}, f32[2,4,2,128]{3,2,1,0:T(2,128)S(1)}, f32[2,4,2,128]{3,2,1,0:T(2,128)S(1)}) fusion(f32[2,4,2,1152]{3,2,1,0:T(2,128)S(1)} %get-tuple-element.92, f32[2,4,2,128]{3,2,1,0:T(2,128)S(1)} %get-tuple-element.338, f32[2,4,2,1152]{3,2,1,0:T(2,128)S(1)} %get-tuple-element.86, ...), kind=kLoop, calls=%fused_computation.163 | loop fusion | flops 110880768 | bytes 680960 | tf_op jit(solution)/shard_map/reduce_sum | solution.py:78
  334.9 21.6 %multiply_reduce_fusion.7 = (f32[2,4,2,128]{3,2,1,0:T(2,128)S(1)}, f32[2,4,2,128]{3,2,1,0:T(2,128)S(1)}, f32[2,4,2,128]{3,2,1,0:T(2,128)S(1)}) fusion(f32[2,4,2,1152]{3,2,1,0:T(2,128)S(1)} %get-tuple-element.100, f32[2,4,2,128]{3,2,1,0:T(2,128)S(1)} %get-tuple-element.338, f32[2,4,2,1152]{3,2,1,0:T(2,128)S(1)} %get-tuple-element.94, ...), kind=kLoop, calls=%fused_computation.182 | loop fusion | flops 113240064 | bytes 680960 | tf_op jit(solution)/shard_map/reduce_sum | solution.py:78
  356.5 21.6 %multiply_reduce_fusion.6 = (f32[2,4,2,128]{3,2,1,0:T(2,128)S(1)}, f32[2,4,2,128]{3,2,1,0:T(2,128)S(1)}, f32[2,4,2,128]{3,2,1,0:T(2,128)S(1)}) fusion(f32[2,4,2,1152]{3,2,1,0:T(2,128)S(1)} %get-tuple-element.108, f32[2,4,2,128]{3,2,1,0:T(2,128)S(1)} %get-tuple-element.338, f32[2,4,2,1152]{3,2,1,0:T(2,128)S(1)} %get-tuple-element.102, ...), kind=kLoop, calls=%fused_computation.170 | loop fusion | flops 113240064 | bytes 680960 | tf_op jit(solution)/shard_map/reduce_sum | solution.py:78
  379.8 3.2 all-to-all-start
  383.1 7.7 all-to-all-done
  392.4 2.9 collective-permute-done.25
  397.2 4.8 collective-permute-start.27
  402.1 3.7 collective-permute-done.27
  406.5 3.0 collective-permute-start.29
  410.8 2.7 collective-permute-start.30
  413.5 6.1 collective-permute-start.31
  421.7 82.1 %all-reduce.6 = (f32[]{:T(128)}, f32[]{:T(128)}) all-reduce(f32[]{:T(128)} %get-tuple-element.78, f32[]{:T(128)} %get-tuple-element.76), channel_id=1, replica_groups=mesh['gx'=8,'gy'=8,'gz'=4] {'gx','gy','gz'}, use_global_device_ids=true, to_apply=%region_41.42 | all-reduce | flops 2 | bytes 16 | tf_op jit(solution)/shard_map/psum | solution.py:132
  505.8 74.6 %psum.58 = f32[]{:T(128)} all-reduce(f32[]{:T(128)} %multiply_reduce_fusion.39), channel_id=1, replica_groups=mesh['gx'=8,'gy'=8,'gz'=4] {'gx','gy','gz'}, use_global_device_ids=true, to_apply=%region_45.46 | all-reduce | flops 1 | bytes 8 | tf_op jit(solution)/shard_map/psum | solution.py:132
  581.8 2.9 collective-permute-start.33
  586.0 2.2 collective-permute-start.34
  588.2 6.7 collective-permute-start.35
  596.9 78.1 %psum.59 = f32[]{:T(128)} all-reduce(f32[]{:T(128)} %get-tuple-element.74), channel_id=1, replica_groups=mesh['gx'=8,'gy'=8,'gz'=4] {'gx','gy','gz'}, use_global_device_ids=true, to_apply=%region_47.48 | all-reduce | flops 1 | bytes 8 | tf_op jit(solution)/shard_map/psum | solution.py:132
  676.9 74.8 %psum.60 = f32[]{:T(128)} all-reduce(f32[]{:T(128)} %get-tuple-element.72), channel_id=1, replica_groups=mesh['gx'=8,'gy'=8,'gz'=4] {'gx','gy','gz'}, use_global_device_ids=true, to_apply=%region_49.50 | all-reduce | flops 1 | bytes 8 | tf_op jit(solution)/shard_map/psum | solution.py:132
  753.1 2.9 collective-permute-start.37
  757.4 2.2 collective-permute-start.38
  759.5 6.7 collective-permute-start.39
  768.3 77.6 %psum.61 = f32[]{:T(128)} all-reduce(f32[]{:T(128)} %get-tuple-element.70), channel_id=1, replica_groups=mesh['gx'=8,'gy'=8,'gz'=4] {'gx','gy','gz'}, use_global_device_ids=true, to_apply=%region_51.52 | all-reduce | flops 1 | bytes 8 | tf_op jit(solution)/shard_map/psum | solution.py:132
  847.8 74.8 %psum.62 = f32[]{:T(128)} all-reduce(f32[]{:T(128)} %multiply_reduce_fusion.35), channel_id=1, replica_groups=mesh['gx'=8,'gy'=8,'gz'=4] {'gx','gy','gz'}, use_global_device_ids=true, to_apply=%region_53.54 | all-reduce | flops 1 | bytes 8 | tf_op jit(solution)/shard_map/psum | solution.py:132
  924.0 2.9 collective-permute-start.41
  928.3 2.2 collective-permute-start.42
  930.4 6.7 collective-permute-start.43
  939.2 77.6 %psum.63 = f32[]{:T(128)} all-reduce(f32[]{:T(128)} %fusion.273), channel_id=1, replica_groups=mesh['gx'=8,'gy'=8,'gz'=4] {'gx','gy','gz'}, use_global_device_ids=true, to_apply=%region_55.56 | all-reduce | flops 1 | bytes 8 | tf_op jit(solution)/shard_map/psum | solution.py:132
  1018.2 2.9 collective-permute-start.45
  1022.4 2.2 collective-permute-start.46
  1024.6 6.7 collective-permute-start.47
  1032.9 19.6 %all_to_all.21 = f32[3,2,1,16]{0,1,2,3:T(2,128)S(1)} all-to-all(f32[3,2,1,16]{0,1,2,3:T(2,128)S(1)} %copy.115), channel_id=1, replica_groups=mesh['gx'=8,'gy'=8,'gz'=4] {'gz'}, dimensions={3} | all-to-all | bytes 768 | tf_op jit(solution)/shard_map/all_to_all | solution.py:170
  (231 shorter events, 51.5 us)
Async XLA Ops:
  3.1 4.6 collective-permute-start
  3.1 4.5 collective-permute-start.1
  7.7 5.9 collective-permute-start.2
  11.2 7.9 collective-permute-start.3
  19.4 7.4 collective-permute-start.4
  24.6 8.1 collective-permute-start.5
  34.3 0.7 copy-start.1
  34.3 0.7 copy-start.2
  56.1 43.2 %copy-start.3 = (f32[3,2,4,2,128]{4,3,2,1,0:T(2,128)S(1)}, f32[3,2,4,2,128]{4,3,2,1,0:T(2,128)}, u32[]{:S(2)}) copy-start(f32[3,2,4,2,128]{4,3,2,1,0:T(2,128)} %param.17) | copy-start | bytes 73732
  56.1 43.2 %copy-start.4 = (f32[3,2,4,2,128]{4,3,2,1,0:T(2,128)S(1)}, f32[3,2,4,2,128]{4,3,2,1,0:T(2,128)}, u32[]{:S(2)}) copy-start(f32[3,2,4,2,128]{4,3,2,1,0:T(2,128)} %param.18) | copy-start | bytes 73732
  99.5 4.6 collective-permute-start.6
  99.5 4.5 collective-permute-start.7
  104.1 5.9 collective-permute-start.8
  106.8 7.9 collective-permute-start.9
  115.0 7.5 collective-permute-start.10
  120.3 7.4 collective-permute-start.11
  150.6 43.2 %copy-start.5 = (f32[3,2,4,2,128]{4,3,2,1,0:T(2,128)S(1)}, f32[3,2,4,2,128]{4,3,2,1,0:T(2,128)}, u32[]{:S(2)}) copy-start(f32[3,2,4,2,128]{4,3,2,1,0:T(2,128)} %param.16) | copy-start | bytes 73732
  193.9 118.8 %copy-start = (f32[3,2,4,2,128]{4,3,2,1,0:T(2,128)}, f32[3,2,4,2,128]{4,3,2,1,0:T(2,128)S(1)}, u32[]{:S(2)}) copy-start(f32[3,2,4,2,128]{4,3,2,1,0:T(2,128)S(1)} %get-tuple-element.310) | copy-start | bytes 73732
  194.0 4.6 collective-permute-start.12
  194.0 4.5 collective-permute-start.13
  198.7 5.9 collective-permute-start.14
  201.2 7.9 collective-permute-start.15
  209.3 5.8 collective-permute-start.16
  212.9 7.4 collective-permute-start.17
  264.9 24.7 %copy-start.8 = (s32[2,4,2,128]{3,2,1,0:T(2,128)S(1)}, s32[2,4,2,128]{3,2,1,0:T(2,128)}, u32[]{:S(2)}) copy-start(s32[2,4,2,128]{3,2,1,0:T(2,128)} %param.21) | copy-start | bytes 24580
  286.6 4.6 collective-permute-start.18
  286.6 4.5 collective-permute-start.19
  291.3 5.9 collective-permute-start.20
  293.5 7.9 collective-permute-start.21
  301.7 5.0 collective-permute-start.22
  304.5 7.4 collective-permute-start.23
  356.5 26.6 %copy-start.10 = (s32[2,1,16]{2,1,0:T(1,128)S(1)}, s32[2,1,16]{2,1,0:T(1,128)}, u32[]{:S(2)}) copy-start(s32[2,1,16]{2,1,0:T(1,128)} %param.23) | copy-start | bytes 388
  356.5 34.5 %copy-start.9 = (f32[3,2,1,16]{3,2,1,0:T(1,128)S(1)}, f32[3,2,1,16]{3,2,1,0:T(1,128)}, u32[]{:S(2)}) copy-start(f32[3,2,1,16]{3,2,1,0:T(1,128)} %param.22) | copy-start | bytes 1156
  379.8 11.0 %all-to-all-start = ((f32[4,2,4,4]{3,1,0,2:T(2,128)}), f32[4,2,4,4]{3,1,0,2:T(2,128)S(1)}, u32[]{:S(2)}, u32[]{:S(2)}) async-start(f32[4,2,4,4]{3,1,0,2:T(2,128)} %copy.107), calls=%async_computation | async-start | bytes 32768 | tf_op jit(solution)/shard_map/all_to_all | solution.py:167
  391.0 1.3 collective-permute-start.24
  391.1 4.2 collective-permute-start.25
  395.3 6.8 collective-permute-start.26
  397.2 8.5 collective-permute-start.27
  406.5 4.2 collective-permute-start.28
  406.5 4.2 collective-permute-start.29
  410.8 8.9 collective-permute-start.30
  413.5 7.4 collective-permute-start.31
  581.8 4.2 collective-permute-start.32
  581.8 4.2 collective-permute-start.33
  586.0 8.9 collective-permute-start.34
  588.2 8.0 collective-permute-start.35
  753.1 4.2 collective-permute-start.36
  753.1 4.2 collective-permute-start.37
  757.4 8.9 collective-permute-start.38
  759.5 8.0 collective-permute-start.39
  924.0 4.2 collective-permute-start.40
  924.0 4.2 collective-permute-start.41
  928.3 8.9 collective-permute-start.42
  930.4 8.0 collective-permute-start.43
  1018.1 35.0 %copy-start.6 = (f32[2,1,16]{2,0,1:T(2,128)}, f32[2,1,16]{2,0,1:T(2,128)S(1)}, u32[]{:S(2)}) copy-start(f32[2,1,16]{2,0,1:T(2,128)S(1)} %fusion.271) | copy-start | bytes 388
  1018.2 4.2 collective-permute-start.44
  1018.2 4.2 collective-permute-start.45
  1022.4 8.9 collective-permute-start.46
  1024.6 8.0 collective-permute-start.47
  1032.8 20.4 %copy-start.7 = (f32[3,2,1,16]{3,1,0,2:T(2,128)}, f32[3,2,1,16]{3,1,0,2:T(2,128)S(1)}, u32[]{:S(2)}) copy-start(f32[3,2,1,16]{3,1,0,2:T(2,128)S(1)} %fusion.257) | copy-start | bytes 1156
where the time goes:
time: 1060 us; the launch traced here: 1050 us
  blocking collectives  559 us (53%)
  other arithmetic  270 us (25%)
  starting transfers between devices  127 us (12%)
  waiting for transfers between devices  77.2 us (7%)
  between operations  11.4 us (1%)
    psum x7, blocking collectives, global_total(): return lax.psum(jnp.sum(values), ('gx', 'gy', 'gz'))  540 us
    reduce_sum x12, other arithmetic, pair_sum(): jnp.sum(strength * deltas[axis_k], axis=-1)  257 us
    ppermute x24, starting transfers between devices, with_halo(): lax.ppermute(lax.slice_in_dim(block, 0, width, axis=dim), axis, backward)  79.6 us
    ppermute x24, waiting for transfers between devices, with_halo(): lax.ppermute(lax.slice_in_dim(block, 0, width, axis=dim), axis, backward)  48 us
    ppermute x24, starting transfers between devices, with_halo(): lax.ppermute(lax.slice_in_dim(block, block.shape[dim] - width, None, axis...  44.5 us
    ppermute x24, waiting for transfers between devices, with_halo(): lax.ppermute(lax.slice_in_dim(block, block.shape[dim] - width, None, axis...  21.5 us
  transfers between devices with their start and end apart: 49, of which 30 were waited for; matrix products, arithmetic and copies ran while one was open for 0% of the time, Pallas kernels for 0%

commit v1 on v0

v1 whole, which is shorter than its diff:
```python
import math

import jax
import jax.numpy as jnp
from jax import lax
from jax.experimental import pallas as pl
from jax.experimental.pallas import tpu as pltpu
from jax.sharding import PartitionSpec as P

STEPS = 2
ITERS = 4

cell_edge = 3.0
conserve = 25.0
friction = 4.5
noise_scale = 3.0 * math.sqrt(12.0) / math.sqrt(0.04)
time_step = 0.04
predict_weight = 0.65
couple_rate = 0.5
hash_prime = 4093.0

ROUND = 12582912.0
SLOTS = 128
IB = 32
NFEAT = 64
HX, HY, HZ = 4, 6, 4
FAR = 1.0e5
damp = -friction / noise_scale
lift = conserve / noise_scale - 0.5 / hash_prime


def rint(value):
    return (value + ROUND) - ROUND


def split3(value):
    hi = value.astype(jnp.bfloat16).astype(jnp.float32)
    rest = value - hi
    mid = rest.astype(jnp.bfloat16).astype(jnp.float32)
    low = (rest - mid).astype(jnp.bfloat16).astype(jnp.float32)
    return hi, mid, low


def rows_of(row, values, default):
    out = default
    for index, value in values:
        out = jnp.where(row == index, value, out)
    return out


def bead_tile(raw, off, row):
    x = raw[0:1] + off[0]
    y = raw[1:2] + off[1]
    z = raw[2:3] + off[2]
    vx = raw[3:4] * damp
    vy = raw[4:5] * damp
    vz = raw[5:6] * damp
    q = x * x + y * y + z * z
    p = x * vx + y * vy + z * vz
    q = jnp.where(raw[7:8] > 0.5, q, FAR)
    return x, y, z, vx, vy, vz, q, p


def centred(seed, tag):
    a = seed + tag
    return jnp.where(a > 2046.0, a - hash_prime, a)


def force_kernel(tag, mode, count_ref, own, zlo, zhi, ylo, yhi, xlo, xhi, *rest):
    if mode == "predict":
        vf, out, feat, posb, left, acc = rest
    elif mode == "step":
        vf, out, vf_out, feat, posb, left, acc = rest
    else:
        vf, half, pos_out, vel_out, bins_out, feat, posb, left, acc = rest
    row8 = lax.broadcasted_iota(jnp.int32, (8, SLOTS), 0)
    row16 = lax.broadcasted_iota(jnp.int32, (16, SLOTS), 0)

    def features(raw, hx, hy, hz):
        off = (
            (hx * 3 - 6).astype(jnp.float32),
            (hy * 3 - 9).astype(jnp.float32),
            (hz * 3 - 6).astype(jnp.float32),
        )
        x, y, z, vx, vy, vz, q, p = bead_tile(raw, off, row8)
        tile = jnp.concatenate([x, y, z, vx, vy, vz, q, p], axis=0)
        hi, mid, low = split3(tile)
        a = centred(raw[6:7], tag)
        c = rint(a * (1.0 / 64.0))
        d = a - 64.0 * c
        fixed = jnp.where(
            row16 < 3, c, jnp.where(row16 < 6, d, jnp.where(row16 < 9, 1.0, 0.0))
        )
        both = jnp.concatenate([hi, mid, hi, low, hi, mid, fixed], axis=0)
        column = pl.multiple_of(((hx * HY + hy) * HZ + hz) * SLOTS, SLOTS)
        feat[:, pl.ds(column, SLOTS)] = both.astype(jnp.bfloat16)
        posb[:, pl.ds(column, SLOTS)] = jnp.concatenate(
            [
                jnp.broadcast_to(x, (8, SLOTS)),
                jnp.broadcast_to(y, (8, SLOTS)),
                jnp.broadcast_to(z, (8, SLOTS)),
            ],
            axis=0,
        )
        return hi, mid, low, tile, a

    def of_own(index, carry):
        hx, hy, hz = index // 8, (index // 2) % 4, index % 2
        raw = own[index]
        hi, mid, low, tile, a = features(raw, hx + 1, hy + 1, hz + 1)
        zero = jnp.zeros((1, SLOTS), jnp.float32)
        one = jnp.ones((1, SLOTS), jnp.float32)

        def s_group(part, last):
            return jnp.concatenate([2.0 * part[0:3], zero, zero, zero, last, zero], axis=0)

        def c_group(part, last):
            return jnp.concatenate([-part[3:6], -part[0:3], zero, last], axis=0)

        x, y, z = tile[0:1], tile[1:2], tile[2:3]
        g3 = split3(1.0 - (x * x + y * y + z * z))
        e3 = split3(tile[7:8])
        a64 = 64.0 * a
        a64 = a64 - hash_prime * rint(a64 * (1.0 / hash_prime))
        b64 = split3(a64 / hash_prime)
        b1 = split3(a / hash_prime)
        shift = split3(jnp.full((1, SLOTS), (0.5 - tag * tag) / hash_prime - 0.5, jnp.float32))
        pad7 = jnp.zeros((7, SLOTS), jnp.float32)
        pad6 = jnp.zeros((6, SLOTS), jnp.float32)
        left_s = jnp.concatenate(
            [
                s_group(hi, -one),
                s_group(hi, -one),
                s_group(mid, zero),
                s_group(hi, -one),
                s_group(low, zero),
                s_group(mid, zero),
                pad6,
                g3[0],
                g3[1],
                g3[2],
                pad7,
            ],
            axis=0,
        )
        left_c = jnp.concatenate(
            [
                c_group(hi, one),
                c_group(hi, one),
                c_group(mid, zero),
                c_group(hi, one),
                c_group(low, zero),
                c_group(mid, zero),
                pad6,
                e3[0],
                e3[1],
                e3[2],
                pad7,
            ],
            axis=0,
        )
        left_u = jnp.concatenate(
            [
                jnp.zeros((48, SLOTS), jnp.float32),
                b64[0],
                b64[1],
                b64[2],
                b1[0],
                b1[1],
                b1[2],
                shift[0],
                shift[1],
                shift[2],
                pad7,
            ],
            axis=0,
        )
        for which, rows in enumerate((left_s, left_c, left_u)):
            turned = rows.T.astype(jnp.bfloat16)
            for block in range(SLOTS // IB):
                start = pl.multiple_of(index * (3 * SLOTS) + (block * 3 + which) * IB, IB)
                left[pl.ds(start, IB), :] = turned[block * IB : (block + 1) * IB]
        return carry

    lax.fori_loop(0, 16, of_own, 0)

    def of_face(ref, count, place):
        def body(index, carry):
            features(ref[index], *place(index))
            return carry

        lax.fori_loop(0, count, body, 0, unroll=2)

    def fixed(value, like):
        return like * 0 + value

    of_face(zlo, 8, lambda i: (i // 4 + 1, i % 4 + 1, fixed(0, i)))
    of_face(zhi, 8, lambda i: (i // 4 + 1, i % 4 + 1, fixed(3, i)))
    of_face(ylo, 8, lambda i: (i // 4 + 1, fixed(0, i), i % 4))
    of_face(yhi, 8, lambda i: (i // 4 + 1, fixed(5, i), i % 4))
    of_face(xlo, 24, lambda i: (fixed(0, i), i // 4, i % 4))
    of_face(xhi, 24, lambda i: (fixed(3, i), i // 4, i % 4))

    def of_cell(index, carry):
        cx, cy, cz = index // 8, (index // 2) % 4, index % 2
        n_own = count_ref[index]
        acc[...] = jnp.zeros_like(acc)

        def of_block(block, inner):
            start = pl.multiple_of(index * (3 * SLOTS) + block * (3 * IB), 3 * IB)
            lhs = left[pl.ds(start, 3 * IB), :]
            sums = [jnp.zeros((IB, SLOTS), jnp.float32) for _ in range(4)]
            columns = [
                pl.multiple_of(
                    (((cx + ox) * HY + (cy + oy)) * HZ + cz) * SLOTS, SLOTS
                )
                for ox in range(3)
                for oy in range(3)
            ]
            groups = [columns[0:2], columns[2:4], columns[4:6], columns[6:8], columns[8:9]]
            for group in groups:
                rhs = jnp.concatenate([feat[:, pl.ds(c, 3 * SLOTS)] for c in group], axis=1)
                forms = jnp.dot(lhs, rhs, preferred_element_type=jnp.float32)
                for piece in range(len(group) * 3):
                    lanes = slice(piece * SLOTS, (piece + 1) * SLOTS)
                    s = forms[0:IB, lanes]
                    damped = forms[IB : 2 * IB, lanes]
                    u = forms[2 * IB : 3 * IB, lanes]
                    weight = jnp.maximum(s, 0.0)
                    strength = weight * ((u - rint(u)) + lift + weight * damped)
                    where = group[piece // 3] + (piece % 3) * SLOTS
                    here = posb[:, pl.ds(pl.multiple_of(where, SLOTS), SLOTS)]
                    for k in range(3):
                        wide = jnp.concatenate([here[8 * k : 8 * k + 8]] * (IB // 8), axis=0)
                        sums[k] = sums[k] + strength * wide
                    sums[3] = sums[3] + strength
            for k in range(4):
                acc[k, pl.ds(pl.multiple_of(block * IB, IB), IB), :] = sums[k]
            return inner

        lax.fori_loop(0, (n_own + (IB - 1)) // IB, of_block, 0)
        moments = [jnp.sum(acc[k].T, axis=0, keepdims=True) for k in range(4)]
        raw = own[index]
        occupied = raw[7:8]
        off = (
            (cx * 3 - 3).astype(jnp.float32),
            (cy * 3 - 6).astype(jnp.float32),
            (cz * 3 - 3).astype(jnp.float32),
        )
        total = [
            noise_scale * occupied * ((raw[k : k + 1] + off[k]) * moments[3] - moments[k])
            for k in range(3)
        ]
        state = vf[index]
        v = [state[k : k + 1] for k in range(3)]
        f = [state[k + 3 : k + 4] for k in range(3)]
        new_v = [v[k] + 0.5 * time_step * (f[k] + total[k]) for k in range(3)]
        if mode == "predict":
            out[index] = jnp.concatenate([raw[0:3], *new_v, raw[6:8]], axis=0)
        elif mode == "step":
            moved = [
                raw[k : k + 1] + time_step * new_v[k] + 0.5 * time_step * time_step * total[k]
                for k in range(3)
            ]
            guess = [new_v[k] + predict_weight * time_step * total[k] for k in range(3)]
            out[index] = jnp.concatenate([*moved, *guess, raw[6:8]], axis=0)
            vf_out[index] = jnp.concatenate([*new_v, *total, raw[6:8]], axis=0)
        else:
            for k in range(3):
                pos_out[k, cx, cy, pl.ds(cz, 1), :] = raw[k : k + 1]
                vel_out[k, cx, cy, pl.ds(cz, 1), :] = new_v[k]
            side = half[cx, cy, pl.ds(cz, 1), :]
            rows = []
            for h in (0, 1):
                select = jnp.where(side == h, occupied, 0.0)
                rows += [new_v[0] * select, new_v[1] * select, new_v[2] * select, select]
            summed = jnp.sum(jnp.concatenate(rows, axis=0), axis=1, keepdims=True)
            lane = lax.broadcasted_iota(jnp.int32, (8, SLOTS), 1)
            bins_out[...] = jnp.where(lane == index, summed, bins_out[...])
        return carry

    if mode == "last":
        bins_out[...] = jnp.zeros_like(bins_out)
    lax.fori_loop(0, 16, of_cell, 0)


def force_call(tag, mode, counts, own, faces, *extra):
    tile = jax.ShapeDtypeStruct((16, 8, SLOTS), jnp.float32)
    bead = jax.ShapeDtypeStruct((3, 2, 4, 2, SLOTS), jnp.float32)
    shapes = {
        "predict": tile,
        "step": (tile, tile),
        "last": (bead, bead, jax.ShapeDtypeStruct((8, SLOTS), jnp.float32)),
    }[mode]
    vmem = pl.BlockSpec(memory_space=pltpu.VMEM)
    n_out = 1 if mode == "predict" else len(shapes)

    def body(*refs):
        force_kernel(float(tag), mode, *refs)

    return pl.pallas_call(
        body,
        out_shape=shapes,
        in_specs=[pl.BlockSpec(memory_space=pltpu.SMEM)] + [vmem] * (7 + len(extra)),
        out_specs=vmem if n_out == 1 else tuple([vmem] * n_out),
        scratch_shapes=[
            pltpu.VMEM((NFEAT, HX * HY * HZ * SLOTS), jnp.bfloat16),
            pltpu.VMEM((24, HX * HY * HZ * SLOTS), jnp.float32),
            pltpu.VMEM((16 * 3 * SLOTS, NFEAT), jnp.bfloat16),
            pltpu.VMEM((4, SLOTS, SLOTS), jnp.float32),
        ],
        cost_estimate=pl.CostEstimate(
            flops=10_000_000, bytes_accessed=1_000_000, transcendentals=0
        ),
        name="pair_" + mode,
    )(counts, own, *faces, *extra)


def shifted(block, axis, periodic, up):
    count = lax.axis_size(axis)
    pairs = [(i, i + 1) for i in range(count - 1)]
    if periodic:
        pairs.append((count - 1, 0))
    if not up:
        pairs = [(b, a) for a, b in pairs]
    return lax.ppermute(block, axis, pairs)


def gather_faces(own):
    zlo = shifted(own[:, :, 1:2], "gz", False, True)
    zhi = shifted(own[:, :, 0:1], "gz", False, False)
    wide_z = jnp.concatenate([zlo, own, zhi], axis=2)
    ylo = shifted(wide_z[:, 3:4], "gy", False, True)
    yhi = shifted(wide_z[:, 0:1], "gy", False, False)
    wide_y = jnp.concatenate([ylo, wide_z, yhi], axis=1)
    xlo = shifted(wide_y[1:2], "gx", True, True)
    xhi = shifted(wide_y[0:1], "gx", True, False)
    return tuple(face.reshape(-1, 8, SLOTS) for face in (zlo, zhi, ylo, yhi, xlo, xhi))


def neighbours(field):
    nx = jnp.roll(field, -1, axis=-3)
    px = jnp.roll(field, 1, axis=-3)
    wide = jnp.pad(field, [(0, 0)] * (field.ndim - 2) + [(1, 1), (1, 1)])
    ny = wide[..., 2:, 1:-1]
    py = wide[..., :-2, 1:-1]
    nz = wide[..., 1:-1, 2:]
    pz = wide[..., 1:-1, :-2]
    return nx, px, ny, py, nz, pz


def project(coupled):
    near = [neighbours(coupled[k]) for k in range(3)]
    residual = -0.5 * (
        near[0][0] - near[0][1] + near[1][2] - near[1][3] + near[2][4] - near[2][5]
    )
    direction = residual
    pressure = jnp.zeros_like(residual)
    norm_now = jnp.sum(residual * residual)
    for repeat in range(ITERS):
        around = neighbours(direction)
        applied = 6.0 * direction - sum(around[1:], around[0])
        step_length = norm_now / jnp.sum(direction * applied)
        pressure = pressure + step_length * direction
        residual = residual - step_length * applied
        norm_next = jnp.sum(residual * residual)
        direction = residual + norm_next / norm_now * direction
        norm_now = norm_next
    nx, px, ny, py, nz, pz = neighbours(pressure)
    gradient = jnp.stack([nx - px, ny - py, nz - pz])
    return coupled - 0.5 * gradient, pressure


def per_device(
    bead_pos, bead_vel, bead_force, cell_count, pair_seed, bead_half, grid_vel, correlation_map
):
    occupied = (lax.broadcasted_iota(jnp.int32, pair_seed.shape, 3) < cell_count[..., None]).astype(
        jnp.float32
    )
    seed = pair_seed.astype(jnp.float32)
    position = bead_pos + time_step * bead_vel + 0.5 * time_step * time_step * bead_force
    guessed = bead_vel + predict_weight * time_step * bead_force
    static = jnp.stack([seed, occupied])
    tiles = jnp.moveaxis(jnp.concatenate([position, guessed, static]), 0, -2)
    state = jnp.moveaxis(jnp.concatenate([bead_vel, bead_force, static]), 0, -2)
    state = state.reshape(16, 8, SLOTS)
    counts = cell_count.reshape(16)
    shape = (2, 4, 2, 8, SLOTS)

    for step in range(STEPS):
        tag = step + 3
        tiles = force_call(
            tag, "predict", counts, tiles.reshape(16, 8, SLOTS), gather_faces(tiles), state
        ).reshape(shape)
        if step < STEPS - 1:
            tiles, state = force_call(
                tag, "step", counts, tiles.reshape(16, 8, SLOTS), gather_faces(tiles), state
            )
            tiles = tiles.reshape(shape)
        else:
            position, velocity, bins = force_call(
                tag,
                "last",
                counts,
                tiles.reshape(16, 8, SLOTS),
                gather_faces(tiles),
                state,
                bead_half,
            )
    sent = jnp.concatenate(
        [
            bins[:, :16].reshape(-1),
            grid_vel.reshape(-1),
            correlation_map.astype(jnp.float32).reshape(-1),
        ]
    )
    nx, ny, nz = (lax.axis_size(a) for a in ("gx", "gy", "gz"))
    world = nx * ny * nz
    got = lax.all_to_all(
        jnp.broadcast_to(sent[None], (world, 256)), ("gx", "gy", "gz"), 0, 0, tiled=True
    )
    bin_all = got[:, :128].reshape(nx, ny, nz, 2, 4, 2, 4, 2)
    bin_all = bin_all.transpose(4, 0, 5, 1, 6, 2, 7, 3).reshape(4, 16, 32, 16)
    grid_all = got[:, 128:224].reshape(nx, ny * nz, 3, 2, 16).transpose(2, 0, 3, 1, 4)
    grid_all = grid_all.reshape(3, 16, 32, 16)
    flag_all = got[:, 224:].reshape(nx, ny * nz, 2, 16).transpose(0, 2, 1, 3).reshape(16, 32, 16)
    mean = bin_all[:3] / jnp.maximum(bin_all[3], 1.0)
    coupled = grid_all + couple_rate * flag_all * (mean - grid_all)
    velocity_all, pressure_all = project(coupled)
    ix, iy, iz = (lax.axis_index(a) for a in ("gx", "gy", "gz"))
    grid_velocity = lax.dynamic_slice(
        velocity_all, (0, 2 * ix, iy * nz + iz, 0), (3, 2, 1, 16)
    )
    pressure = lax.dynamic_slice(pressure_all, (2 * ix, iy * nz + iz, 0), (2, 1, 16))
    brick = lax.dynamic_slice(velocity_all, (0, 2 * ix, 4 * iy, 4 * iz), (3, 2, 4, 4))
    return (position, velocity, grid_velocity, pressure, brick)


def solution(mesh):
    placed = (
        P(None, "gx", "gy", "gz", None),
        P(None, "gx", "gy", "gz", None),
        P(None, "gx", "gy", "gz", None),
        P("gx", "gy", "gz"),
        P("gx", "gy", "gz", None),
        P("gx", "gy", "gz", None),
        P(None, "gx", ("gy", "gz"), None),
        P("gx", ("gy", "gz"), None),
    )
    return jax.shard_map(
        per_device,
        mesh=mesh,
        in_specs=placed,
        out_specs=(
            P(None, "gx", "gy", "gz", None),
            P(None, "gx", "gy", "gz", None),
            P(None, "gx", ("gy", "gz"), None),
            P("gx", ("gy", "gz"), None),
            P(None, "gx", "gy", "gz"),
        ),
        check_vma=False,
    )
```

time: 1060 us -> 305 us (0.29)
  blocking collectives: 559 us -> 0 us
  other arithmetic: 270 us -> 14.8 us
  Pallas kernels: 0 us -> 92.5 us
  waiting for transfers between devices: 77.2 us -> 39.3 us
  local copies, waits for them, and re-layouts: 7.86 us -> 42.3 us
  starting transfers between devices: 127 us -> 100 us
    psum x7 -> x0, blocking collectives: 540 us -> none  [global_total(): return lax.psum(jnp.sum(values), ('gx', 'gy', 'gz'))]
    reduce_sum x22 -> x7, other arithmetic: 263 us -> 4.91 us  [the longest x4 3 us: project(): step_length = norm_now / jnp.sum(direction * applied)]
    pallas_call x0 -> x4, Pallas kernels: none -> 92.5 us  [force_call(): pl.pallas_call(body, out_shape=shapes, in_specs=[pl.BlockSpec(memory_spac...]
    ppermute x48 -> x24, waiting for transfers between devices: 69.5 us -> 25.2 us  [shifted(): return lax.ppermute(block, axis, pairs)]
    ppermute x48 -> x24, starting transfers between devices: 124 us -> 79.9 us  [shifted(): return lax.ppermute(block, axis, pairs)]
    all_to_all x1 -> x0, blocking collectives: 19.6 us -> none  [per_device(): lax.all_to_all(grid_velocity, 'gz', split_axis=3, concat_axis=2, tiled=True)]
    all_to_all x1, starting transfers between devices: 3.25 us -> 20.5 us  [per_device(): lax.all_to_all(jnp.broadcast_to(sent[None], (world, 256)), ('gx', 'gy', '...]
    reshape x1 -> x7, local copies, waits for them, and re-layouts: 0.73 us -> 16.2 us  [the longest x2 14.6 us: per_device(): bin_all = got[:, :128].reshape(nx, ny, nz, 2, 4, 2, 4, 2)]
  transfers between devices with their start and end apart: 49 -> 25, of which waited for: 30 -> 15; matrix products, arithmetic and copies ran while one was open for 0% -> 2% of each run, Pallas kernels for 0% -> 0%
where the time goes in v1:
time: 305 us; the launch traced here: 300 us
  starting transfers between devices  100 us (33%)
  Pallas kernels  92.5 us (30%)
  local copies, waits for them, and re-layouts  42.3 us (14%)
  waiting for transfers between devices  39.3 us (13%)
  other arithmetic  14.8 us (5%)
  between operations  10.7 us (4%)
    pallas_call x4, Pallas kernels, force_call(): pl.pallas_call(body, out_shape=shapes, in_specs=[pl.BlockSpec(memory_spac...  92.5 us
    ppermute x24, starting transfers between devices, shifted(): return lax.ppermute(block, axis, pairs)  79.9 us
    ppermute x24, waiting for transfers between devices, shifted(): return lax.ppermute(block, axis, pairs)  25.2 us
    all_to_all x1, starting transfers between devices, per_device(): lax.all_to_all(jnp.broadcast_to(sent[None], (world, 256)), ('gx', 'gy', '...  20.5 us
    reshape x2, local copies, waits for them, and re-layouts, per_device(): bin_all = got[:, :128].reshape(nx, ny, nz, 2, 4, 2, 4, 2)  14.6 us
    all_to_all x1, waiting for transfers between devices, per_device(): lax.all_to_all(jnp.broadcast_to(sent[None], (world, 256)), ('gx', 'gy', '...  14.1 us
    slice x3, local copies, waits for them, and re-layouts, per_device(): mean = bin_all[:3] / jnp.maximum(bin_all[3], 1.0)  7.86 us
  transfers between devices with their start and end apart: 25, of which 15 were waited for; matrix products, arithmetic and copies ran while one was open for 2% of the time, Pallas kernels for 0%

profile of v1, /device:TPU:24, one launch (start us, length us, event | category | flops | bytes accessed | tf_op | source)
XLA Modules:
  0.0 299.9 jit_solution(13531225796157789380)
XLA Ops:
  0.6 0.8 copy.75
  2.2 0.8 multiply_add_fusion.6
  3.0 0.8 fusion.32
  3.9 1.3 collective-permute-start.1
  5.2 5.8 %collective-permute-start = (f32[2,4,1,8,128]{4,2,1,0,3:T(1,128)S(1)}, f32[2,4,1,8,128]{4,2,1,0,3:T(1,128)S(1)}, u32[]{:S(2)}, u32[]{:S(2)}) collective-permute-start(f32[2,4,1,8,128]{4,2,1,0,3:T(1,128)S(1)} %get-tuple-element.97), channel_id=1, source_target_pairs={{0,1},{1,2},{2,3},{4,5},{5,6},{6,7},{8,9},{9,10},{10,11},{12,13},{... | collective-permute-start | bytes 98312 | tf_op jit(solution)/shard_map/ppermute | solution.py:326
  11.0 1.6 collective-permute-done
  12.6 2.7 collective-permute-start.3
  15.3 5.3 %collective-permute-start.2 = (f32[2,1,4,8,128]{4,2,1,0,3:T(4,128)S(1)}, f32[2,1,4,8,128]{4,2,1,0,3:T(4,128)S(1)}, u32[]{:S(2)}, u32[]{:S(2)}) collective-permute-start(f32[2,1,4,8,128]{4,2,1,0,3:T(4,128)S(1)} %get-tuple-element.89), channel_id=1, source_target_pairs={{0,4},{4,8},{8,12},{12,16},{16,20},{20,24},{24,28},{1,5},{5,9},{9,... | collective-permute-start | bytes 98312 | tf_op jit(solution)/shard_map/ppermute | solution.py:326
  20.6 1.6 collective-permute-done.2
  28.5 22.8 %pair_predict.2.refs_1_ = f32[16,8,128]{2,1,0:T(8,128)} custom-call(s32[16]{0:T(128)} %reshape.216.refs_0_, f32[16,8,128]{2,1,0:T(8,128)} %bitcast.108, f32[8,8,128]{2,1,0:T(8,128)} %bitcast.116, f32[8,8,128]{2,1,0:T(8,128)} %bitcast.115, f32[8,8,128]{2,1,0:T(8,128)} %bitcast.118, f32[8,8,128]{2,1,0:T(8,128)} %bitcast.117, f32[24,8,128]{2,1,0:T(8,128)} %bitcast.101, ...), custom_call_target="tpu_custom_call" | custom-call | flops 10000000 | bytes 1000000 | tf_op jit(solution)/shard_map/pair_predict/pallas_call | solution.py:301
  51.3 0.8 fusion.51
  52.0 1.3 collective-permute-start.7
  53.3 5.8 %collective-permute-start.6 = (f32[2,4,1,8,128]{4,3,2,1,0:T(8,128)S(1)}, f32[2,4,1,8,128]{4,3,2,1,0:T(8,128)S(1)}, u32[]{:S(2)}, u32[]{:S(2)}) collective-permute-start(f32[2,4,1,8,128]{4,3,2,1,0:T(8,128)S(1)} %get-tuple-element.95), channel_id=1, source_target_pairs={{0,1},{1,2},{2,3},{4,5},{5,6},{6,7},{8,9},{9,10},{10,11},{12,13},{... | collective-permute-start | bytes 98312 | tf_op jit(solution)/shard_map/ppermute | solution.py:326
  59.2 1.6 collective-permute-done.6
  60.7 0.8 pad_maximum_fusion.14
  61.5 3.7 %collective-permute-start.9 = (f32[2,1,4,8,128]{4,3,2,1,0:T(8,128)S(1)}, f32[2,1,4,8,128]{4,3,2,1,0:T(8,128)S(1)}, u32[]{:S(2)}, u32[]{:S(2)}) collective-permute-start(f32[2,1,4,8,128]{4,3,2,1,0:T(8,128)S(1)} %get-tuple-element.86), channel_id=1, source_target_pairs={{4,0},{8,4},{12,8},{16,12},{20,16},{24,20},{28,24},{5,1},{9,5},{13... | collective-permute-start | bytes 98312 | tf_op jit(solution)/shard_map/ppermute | solution.py:326
  65.2 9.4 %collective-permute-start.8 = (f32[2,1,4,8,128]{4,3,2,1,0:T(8,128)S(1)}, f32[2,1,4,8,128]{4,3,2,1,0:T(8,128)S(1)}, u32[]{:S(2)}, u32[]{:S(2)}) collective-permute-start(f32[2,1,4,8,128]{4,3,2,1,0:T(8,128)S(1)} %get-tuple-element.87), channel_id=1, source_target_pairs={{0,4},{4,8},{8,12},{12,16},{16,20},{20,24},{24,28},{1,5},{5,9},{9,... | collective-permute-start | bytes 98312 | tf_op jit(solution)/shard_map/ppermute | solution.py:326
  74.7 1.6 collective-permute-done.8
  76.2 0.9 pad_maximum_fusion.1
  77.5 0.7 collective-permute-start.10
  78.2 1.5 collective-permute-done.11
  79.7 3.0 %collective-permute-done.10 = f32[1,6,4,8,128]{4,3,2,1,0:T(8,128)S(1)} collective-permute-done((f32[1,6,4,8,128]{4,3,2,1,0:T(8,128)S(1)}, f32[1,6,4,8,128]{4,3,2,1,0:T(8,128)S(1)}, u32[]{:S(2)}, u32[]{:S(2)}) %collective-permute-start.10) | collective-permute-done | bytes 98336 | tf_op jit(solution)/shard_map/ppermute | solution.py:326
  83.4 23.0 %pair_step.1 = (f32[16,8,128]{2,1,0:T(8,128)}, f32[16,8,128]{2,1,0:T(8,128)}) custom-call(s32[16]{0:T(128)} %reshape.216.refs_0_, f32[16,8,128]{2,1,0:T(8,128)} %pair_predict.2.refs_1_, f32[8,8,128]{2,1,0:T(8,128)} %bitcast.106, f32[8,8,128]{2,1,0:T(8,128)} %bitcast.104, f32[8,8,128]{2,1,0:T(8,128)} %bitcast.113, f32[8,8,128]{2,1,0:T(8,128)} %bitcast.111, ...), custom_call_target="tpu_custom_call" | custom-call | flops 10000000 | bytes 1000000 | tf_op jit(solution)/shard_map/pair_step/pallas_call | solution.py:301
  106.3 0.8 fusion.50
  107.1 1.3 collective-permute-start.13
  108.4 6.9 %collective-permute-start.12 = (f32[2,4,1,8,128]{4,3,2,1,0:T(8,128)S(1)}, f32[2,4,1,8,128]{4,3,2,1,0:T(8,128)S(1)}, u32[]{:S(2)}, u32[]{:S(2)}) collective-permute-start(f32[2,4,1,8,128]{4,3,2,1,0:T(8,128)S(1)} %get-tuple-element.93), channel_id=1, source_target_pairs={{0,1},{1,2},{2,3},{4,5},{5,6},{6,7},{8,9},{9,10},{10,11},{12,13},{... | collective-permute-start | bytes 98312 | tf_op jit(solution)/shard_map/ppermute | solution.py:326
  115.3 1.6 collective-permute-done.12
  116.9 0.8 pad_maximum_fusion.11
  117.6 1.9 collective-permute-start.15
  119.5 11.2 %collective-permute-start.14 = (f32[2,1,4,8,128]{4,3,2,1,0:T(8,128)S(1)}, f32[2,1,4,8,128]{4,3,2,1,0:T(8,128)S(1)}, u32[]{:S(2)}, u32[]{:S(2)}) collective-permute-start(f32[2,1,4,8,128]{4,3,2,1,0:T(8,128)S(1)} %get-tuple-element.85), channel_id=1, source_target_pairs={{0,4},{4,8},{8,12},{12,16},{16,20},{20,24},{24,28},{1,5},{5,9},{9,... | collective-permute-start | bytes 98312 | tf_op jit(solution)/shard_map/ppermute | solution.py:326
  130.8 1.6 collective-permute-done.14
  132.4 0.9 pad_maximum_fusion.2
  133.8 1.7 collective-permute-done.17
  135.5 3.1 %collective-permute-done.16 = f32[1,6,4,8,128]{4,3,2,1,0:T(8,128)S(1)} collective-permute-done((f32[1,6,4,8,128]{4,3,2,1,0:T(8,128)S(1)}, f32[1,6,4,8,128]{4,3,2,1,0:T(8,128)S(1)}, u32[]{:S(2)}, u32[]{:S(2)}) %collective-permute-start.16) | collective-permute-done | bytes 98336 | tf_op jit(solution)/shard_map/ppermute | solution.py:326
  139.2 22.8 %pair_predict.3.refs_1_ = f32[16,8,128]{2,1,0:T(8,128)} custom-call(s32[16]{0:T(128)} %reshape.216.refs_0_, f32[16,8,128]{2,1,0:T(8,128)} %get-tuple-element.10.refs_1_, f32[8,8,128]{2,1,0:T(8,128)} %bitcast.107, f32[8,8,128]{2,1,0:T(8,128)} %bitcast.105, f32[8,8,128]{2,1,0:T(8,128)} %bitcast.114, f32[8,8,128]{2,1,0:T(8,128)} %bitcast.112, ...), custom_call_target="tpu_custom_call" | custom-call | flops 10000000 | bytes 1000000 | tf_op jit(solution)/shard_map/pair_predict/pallas_call | solution.py:301
  162.0 0.8 fusion.49
  162.7 1.3 collective-permute-start.19
  164.0 6.2 %collective-permute-start.18 = (f32[2,4,1,8,128]{4,3,2,1,0:T(8,128)S(1)}, f32[2,4,1,8,128]{4,3,2,1,0:T(8,128)S(1)}, u32[]{:S(2)}, u32[]{:S(2)}) collective-permute-start(f32[2,4,1,8,128]{4,3,2,1,0:T(8,128)S(1)} %get-tuple-element.91), channel_id=1, source_target_pairs={{0,1},{1,2},{2,3},{4,5},{5,6},{6,7},{8,9},{9,10},{10,11},{12,13},{... | collective-permute-start | bytes 98312 | tf_op jit(solution)/shard_map/ppermute | solution.py:326
  170.3 1.6 collective-permute-done.18
  171.8 0.8 pad_maximum_fusion.8
  172.6 1.9 collective-permute-start.21
  174.5 11.2 %collective-permute-start.20 = (f32[2,1,4,8,128]{4,3,2,1,0:T(8,128)S(1)}, f32[2,1,4,8,128]{4,3,2,1,0:T(8,128)S(1)}, u32[]{:S(2)}, u32[]{:S(2)}) collective-permute-start(f32[2,1,4,8,128]{4,3,2,1,0:T(8,128)S(1)} %get-tuple-element.83), channel_id=1, source_target_pairs={{0,4},{4,8},{8,12},{12,16},{16,20},{20,24},{24,28},{1,5},{5,9},{9,... | collective-permute-start | bytes 98312 | tf_op jit(solution)/shard_map/ppermute | solution.py:326
  185.8 1.6 collective-permute-done.20
  187.3 0.9 pad_maximum_fusion.3
  190.5 3.1 %collective-permute-done.22 = f32[1,6,4,8,128]{4,3,2,1,0:T(8,128)S(1)} collective-permute-done((f32[1,6,4,8,128]{4,3,2,1,0:T(8,128)S(1)}, f32[1,6,4,8,128]{4,3,2,1,0:T(8,128)S(1)}, u32[]{:S(2)}, u32[]{:S(2)}) %collective-permute-start.22) | collective-permute-done | bytes 98336 | tf_op jit(solution)/shard_map/ppermute | solution.py:326
  194.1 23.9 %pair_last.1 = (f32[3,2,4,2,128]{4,3,2,1,0:T(2,128)}, f32[3,2,4,2,128]{4,3,2,1,0:T(2,128)}, f32[8,128]{1,0:T(8,128)}) custom-call(s32[16]{0:T(128)} %reshape.216.refs_0_, f32[16,8,128]{2,1,0:T(8,128)} %pair_predict.3.refs_1_, f32[8,8,128]{2,1,0:T(8,128)} %bitcast.103, f32[8,8,128]{2,1,0:T(8,128)} %bitcast.102, f32[8,8,128]{2,1,0:T(8,128)} %bitcast.110, ...), custom_call_target="tpu_custom_call" | custom-call | flops 10000000 | bytes 1000000 | tf_op jit(solution)/shard_map/pair_last/pallas_call | solution.py:301
  218.1 0.8 reshape.246
  218.9 0.8 broadcast_in_dim.2
  219.7 20.5 %all-to-all-start = ((f32[256,1,256]{2,1,0:T(1,128)}), f32[256,1,256]{2,1,0:T(1,128)S(1)}, u32[]{:S(2)}, u32[]{:S(2)}) async-start(f32[256,1,256]{2,1,0:T(1,128)} %broadcast_in_dim.2), calls=%async_computation | async-start | bytes 524288 | tf_op jit(solution)/shard_map/all_to_all | solution.py:419
  240.2 14.1 %all-to-all-done = f32[256,1,256]{2,1,0:T(1,128)S(1)} async-done(((f32[256,1,256]{2,1,0:T(1,128)}), f32[256,1,256]{2,1,0:T(1,128)S(1)}, u32[]{:S(2)}, u32[]{:S(2)}) %all-to-all-start) | async-done | bytes 262176 | tf_op jit(solution)/shard_map/all_to_all | solution.py:419
  254.6 5.7 %reshape.251 = f32[8,8,4,2,4,2,4,2]{2,1,0,7,6,5,4,3:T(8,128)} reshape(f32[256,128]{0,1:T(8,128)S(1)} %slice.368) | data formatting | bytes 262144 | tf_op jit(solution)/shard_map/reshape | solution.py:422
  260.2 8.9 %copy.88 = f32[8,8,4,2,4,2,4,2]{1,0,3,7,2,6,5,4:T(8,128)S(1)} copy(f32[8,8,4,2,4,2,4,2]{2,1,0,7,6,5,4,3:T(8,128)} %reshape.251) | data formatting | bytes 262144 | tf_op jit(solution)/shard_map/reshape | solution.py:422
  269.2 1.3 slice.369
  271.4 0.8 copy.86
  272.3 1.6 copy.90
  273.8 1.0 max.15
  274.8 5.7 %copy.89 = f32[3,8,2,8,4,4,2,2]{4,3,7,6,5,2,1,0:T(8,128)S(1)} copy(f32[3,8,2,8,4,4,2,2]{3,1,7,6,5,4,2,0:T(8,128)} %slice.369) | data formatting | bytes 196608 | tf_op jit(solution)/shard_map/slice | solution.py:427
  280.5 0.8 slice.294
  281.3 1.2 multiply_add_fusion
  282.7 0.8 multiply_reduce_fusion.5
  286.9 0.7 multiply_reduce_fusion.3
  291.0 0.8 multiply_reduce_fusion.1
  295.1 0.8 fusion.30
  299.1 0.7 copy.93
  (119 shorter events, 17.5 us)
Async XLA Ops:
  3.9 7.1 %collective-permute-start.1 = (f32[2,4,1,8,128]{4,2,1,0,3:T(1,128)S(1)}, f32[2,4,1,8,128]{4,2,1,0,3:T(1,128)S(1)}, u32[]{:S(2)}, u32[]{:S(2)}) collective-permute-start(f32[2,4,1,8,128]{4,2,1,0,3:T(1,128)S(1)} %get-tuple-element.96), channel_id=1, source_target_pairs={{1,0},{2,1},{3,2},{5,4},{6,5},{7,6},{9,8},{10,9},{11,10},{13,12},{... | collective-permute-start | bytes 98312 | tf_op jit(solution)/shard_map/ppermute | solution.py:326
  5.2 7.4 %collective-permute-start = (f32[2,4,1,8,128]{4,2,1,0,3:T(1,128)S(1)}, f32[2,4,1,8,128]{4,2,1,0,3:T(1,128)S(1)}, u32[]{:S(2)}, u32[]{:S(2)}) collective-permute-start(f32[2,4,1,8,128]{4,2,1,0,3:T(1,128)S(1)} %get-tuple-element.97), channel_id=1, source_target_pairs={{0,1},{1,2},{2,3},{4,5},{5,6},{6,7},{8,9},{9,10},{10,11},{12,13},{... | collective-permute-start | bytes 98312 | tf_op jit(solution)/shard_map/ppermute | solution.py:326
  12.6 8.0 %collective-permute-start.3 = (f32[2,1,4,8,128]{4,2,1,0,3:T(4,128)S(1)}, f32[2,1,4,8,128]{4,2,1,0,3:T(4,128)S(1)}, u32[]{:S(2)}, u32[]{:S(2)}) collective-permute-start(f32[2,1,4,8,128]{4,2,1,0,3:T(4,128)S(1)} %get-tuple-element.88), channel_id=1, source_target_pairs={{4,0},{8,4},{12,8},{16,12},{20,16},{24,20},{28,24},{5,1},{9,5},{13... | collective-permute-start | bytes 98312 | tf_op jit(solution)/shard_map/ppermute | solution.py:326
  15.3 6.9 %collective-permute-start.2 = (f32[2,1,4,8,128]{4,2,1,0,3:T(4,128)S(1)}, f32[2,1,4,8,128]{4,2,1,0,3:T(4,128)S(1)}, u32[]{:S(2)}, u32[]{:S(2)}) collective-permute-start(f32[2,1,4,8,128]{4,2,1,0,3:T(4,128)S(1)} %get-tuple-element.89), channel_id=1, source_target_pairs={{0,4},{4,8},{8,12},{12,16},{16,20},{20,24},{24,28},{1,5},{5,9},{9,... | collective-permute-start | bytes 98312 | tf_op jit(solution)/shard_map/ppermute | solution.py:326
  22.3 4.8 %collective-permute-start.5 = (f32[1,6,4,8,128]{4,2,1,0,3:T(4,128)S(1)}, f32[1,6,4,8,128]{4,2,1,0,3:T(4,128)S(1)}, u32[]{:S(2)}, u32[]{:S(2)}) collective-permute-start(f32[1,6,4,8,128]{4,2,1,0,3:T(4,128)S(1)} %get-tuple-element.58), channel_id=1, source_target_pairs={{32,0},{64,32},{96,64},{128,96},{160,128},{192,160},{224,192},{0,2... | collective-permute-start | bytes 294920 | tf_op jit(solution)/shard_map/ppermute | solution.py:326
  22.5 5.3 %collective-permute-start.4 = (f32[1,6,4,8,128]{4,2,1,0,3:T(4,128)S(1)}, f32[1,6,4,8,128]{4,2,1,0,3:T(4,128)S(1)}, u32[]{:S(2)}, u32[]{:S(2)}) collective-permute-start(f32[1,6,4,8,128]{4,2,1,0,3:T(4,128)S(1)} %get-tuple-element.59), channel_id=1, source_target_pairs={{0,32},{32,64},{64,96},{96,128},{128,160},{160,192},{192,224},{224... | collective-permute-start | bytes 294920 | tf_op jit(solution)/shard_map/ppermute | solution.py:326
  52.0 7.1 %collective-permute-start.7 = (f32[2,4,1,8,128]{4,3,2,1,0:T(8,128)S(1)}, f32[2,4,1,8,128]{4,3,2,1,0:T(8,128)S(1)}, u32[]{:S(2)}, u32[]{:S(2)}) collective-permute-start(f32[2,4,1,8,128]{4,3,2,1,0:T(8,128)S(1)} %get-tuple-element.94), channel_id=1, source_target_pairs={{1,0},{2,1},{3,2},{5,4},{6,5},{7,6},{9,8},{10,9},{11,10},{13,12},{... | collective-permute-start | bytes 98312 | tf_op jit(solution)/shard_map/ppermute | solution.py:326
  53.3 135.4 %copy-start.19 = (s32[2,1,16]{2,1,0:T(1,128)S(1)}, s32[2,1,16]{2,1,0:T(1,128)}, u32[]{:S(2)}) copy-start(s32[2,1,16]{2,1,0:T(1,128)} %param.15) | copy-start | bytes 388
  53.3 136.0 %copy-start.18 = (f32[3,2,1,16]{3,2,1,0:T(1,128)S(1)}, f32[3,2,1,16]{3,2,1,0:T(1,128)}, u32[]{:S(2)}) copy-start(f32[3,2,1,16]{3,2,1,0:T(1,128)} %param.14) | copy-start | bytes 1156
  53.3 7.4 %collective-permute-start.6 = (f32[2,4,1,8,128]{4,3,2,1,0:T(8,128)S(1)}, f32[2,4,1,8,128]{4,3,2,1,0:T(8,128)S(1)}, u32[]{:S(2)}, u32[]{:S(2)}) collective-permute-start(f32[2,4,1,8,128]{4,3,2,1,0:T(8,128)S(1)} %get-tuple-element.95), channel_id=1, source_target_pairs={{0,1},{1,2},{2,3},{4,5},{5,6},{6,7},{8,9},{9,10},{10,11},{12,13},{... | collective-permute-start | bytes 98312 | tf_op jit(solution)/shard_map/ppermute | solution.py:326
  59.1 23.6 %copy-start.2 = (f32[2,4,1,8,128]{4,3,2,1,0:T(8,128)}, f32[2,4,1,8,128]{4,3,2,1,0:T(8,128)S(1)}, u32[]{:S(2)}) copy-start(f32[2,4,1,8,128]{4,3,2,1,0:T(8,128)S(1)} %collective-permute-done.7) | copy-start | bytes 98308
  60.7 22.0 %copy-start.4 = (f32[2,4,1,8,128]{4,3,2,1,0:T(8,128)}, f32[2,4,1,8,128]{4,3,2,1,0:T(8,128)S(1)}, u32[]{:S(2)}) copy-start(f32[2,4,1,8,128]{4,3,2,1,0:T(8,128)S(1)} %collective-permute-done.6) | copy-start | bytes 98308
  61.5 13.2 %collective-permute-start.9 = (f32[2,1,4,8,128]{4,3,2,1,0:T(8,128)S(1)}, f32[2,1,4,8,128]{4,3,2,1,0:T(8,128)S(1)}, u32[]{:S(2)}, u32[]{:S(2)}) collective-permute-start(f32[2,1,4,8,128]{4,3,2,1,0:T(8,128)S(1)} %get-tuple-element.86), channel_id=1, source_target_pairs={{4,0},{8,4},{12,8},{16,12},{20,16},{24,20},{28,24},{5,1},{9,5},{13... | collective-permute-start | bytes 98312 | tf_op jit(solution)/shard_map/ppermute | solution.py:326
  65.2 11.0 %collective-permute-start.8 = (f32[2,1,4,8,128]{4,3,2,1,0:T(8,128)S(1)}, f32[2,1,4,8,128]{4,3,2,1,0:T(8,128)S(1)}, u32[]{:S(2)}, u32[]{:S(2)}) collective-permute-start(f32[2,1,4,8,128]{4,3,2,1,0:T(8,128)S(1)} %get-tuple-element.87), channel_id=1, source_target_pairs={{0,4},{4,8},{8,12},{12,16},{16,20},{20,24},{24,28},{1,5},{5,9},{9,... | collective-permute-start | bytes 98312 | tf_op jit(solution)/shard_map/ppermute | solution.py:326
  74.7 8.1 %copy-start.8 = (f32[2,1,4,8,128]{4,3,2,1,0:T(8,128)}, f32[2,1,4,8,128]{4,3,2,1,0:T(8,128)S(1)}, u32[]{:S(2)}) copy-start(f32[2,1,4,8,128]{4,3,2,1,0:T(8,128)S(1)} %collective-permute-done.9) | copy-start | bytes 98308
  76.2 6.5 %copy-start.10 = (f32[2,1,4,8,128]{4,3,2,1,0:T(8,128)}, f32[2,1,4,8,128]{4,3,2,1,0:T(8,128)S(1)}, u32[]{:S(2)}) copy-start(f32[2,1,4,8,128]{4,3,2,1,0:T(8,128)S(1)} %collective-permute-done.8) | copy-start | bytes 98308
  77.1 2.5 collective-permute-start.11
  77.5 5.3 %collective-permute-start.10 = (f32[1,6,4,8,128]{4,3,2,1,0:T(8,128)S(1)}, f32[1,6,4,8,128]{4,3,2,1,0:T(8,128)S(1)}, u32[]{:S(2)}, u32[]{:S(2)}) collective-permute-start(f32[1,6,4,8,128]{4,3,2,1,0:T(8,128)S(1)} %get-tuple-element.57), channel_id=1, source_target_pairs={{0,32},{32,64},{64,96},{96,128},{128,160},{160,192},{192,224},{224... | collective-permute-start | bytes 294920 | tf_op jit(solution)/shard_map/ppermute | solution.py:326
  79.7 3.1 %copy-start.16 = (f32[1,6,4,8,128]{4,3,2,1,0:T(8,128)}, f32[1,6,4,8,128]{4,3,2,1,0:T(8,128)S(1)}, u32[]{:S(2)}) copy-start(f32[1,6,4,8,128]{4,3,2,1,0:T(8,128)S(1)} %collective-permute-done.11) | copy-start | bytes 294916
  82.7 0.6 copy-start.17
  107.1 8.2 %collective-permute-start.13 = (f32[2,4,1,8,128]{4,3,2,1,0:T(8,128)S(1)}, f32[2,4,1,8,128]{4,3,2,1,0:T(8,128)S(1)}, u32[]{:S(2)}, u32[]{:S(2)}) collective-permute-start(f32[2,4,1,8,128]{4,3,2,1,0:T(8,128)S(1)} %get-tuple-element.92), channel_id=1, source_target_pairs={{1,0},{2,1},{3,2},{5,4},{6,5},{7,6},{9,8},{10,9},{11,10},{13,12},{... | collective-permute-start | bytes 98312 | tf_op jit(solution)/shard_map/ppermute | solution.py:326
  108.4 8.5 %collective-permute-start.12 = (f32[2,4,1,8,128]{4,3,2,1,0:T(8,128)S(1)}, f32[2,4,1,8,128]{4,3,2,1,0:T(8,128)S(1)}, u32[]{:S(2)}, u32[]{:S(2)}) collective-permute-start(f32[2,4,1,8,128]{4,3,2,1,0:T(8,128)S(1)} %get-tuple-element.93), channel_id=1, source_target_pairs={{0,1},{1,2},{2,3},{4,5},{5,6},{6,7},{8,9},{9,10},{10,11},{12,13},{... | collective-permute-start | bytes 98312 | tf_op jit(solution)/shard_map/ppermute | solution.py:326
  115.3 23.2 %copy-start.3 = (f32[2,4,1,8,128]{4,3,2,1,0:T(8,128)}, f32[2,4,1,8,128]{4,3,2,1,0:T(8,128)S(1)}, u32[]{:S(2)}) copy-start(f32[2,4,1,8,128]{4,3,2,1,0:T(8,128)S(1)} %collective-permute-done.13) | copy-start | bytes 98308
  116.9 21.7 %copy-start.5 = (f32[2,4,1,8,128]{4,3,2,1,0:T(8,128)}, f32[2,4,1,8,128]{4,3,2,1,0:T(8,128)S(1)}, u32[]{:S(2)}) copy-start(f32[2,4,1,8,128]{4,3,2,1,0:T(8,128)S(1)} %collective-permute-done.12) | copy-start | bytes 98308
  117.6 13.2 %collective-permute-start.15 = (f32[2,1,4,8,128]{4,3,2,1,0:T(8,128)S(1)}, f32[2,1,4,8,128]{4,3,2,1,0:T(8,128)S(1)}, u32[]{:S(2)}, u32[]{:S(2)}) collective-permute-start(f32[2,1,4,8,128]{4,3,2,1,0:T(8,128)S(1)} %get-tuple-element.84), channel_id=1, source_target_pairs={{4,0},{8,4},{12,8},{16,12},{20,16},{24,20},{28,24},{5,1},{9,5},{13... | collective-permute-start | bytes 98312 | tf_op jit(solution)/shard_map/ppermute | solution.py:326
  119.5 12.8 %collective-permute-start.14 = (f32[2,1,4,8,128]{4,3,2,1,0:T(8,128)S(1)}, f32[2,1,4,8,128]{4,3,2,1,0:T(8,128)S(1)}, u32[]{:S(2)}, u32[]{:S(2)}) collective-permute-start(f32[2,1,4,8,128]{4,3,2,1,0:T(8,128)S(1)} %get-tuple-element.85), channel_id=1, source_target_pairs={{0,4},{4,8},{8,12},{12,16},{16,20},{20,24},{24,28},{1,5},{5,9},{9,... | collective-permute-start | bytes 98312 | tf_op jit(solution)/shard_map/ppermute | solution.py:326
  130.8 7.8 %copy-start.9 = (f32[2,1,4,8,128]{4,3,2,1,0:T(8,128)}, f32[2,1,4,8,128]{4,3,2,1,0:T(8,128)S(1)}, u32[]{:S(2)}) copy-start(f32[2,1,4,8,128]{4,3,2,1,0:T(8,128)S(1)} %collective-permute-done.15) | copy-start | bytes 98308
  132.4 6.2 %copy-start.11 = (f32[2,1,4,8,128]{4,3,2,1,0:T(8,128)}, f32[2,1,4,8,128]{4,3,2,1,0:T(8,128)S(1)}, u32[]{:S(2)}) copy-start(f32[2,1,4,8,128]{4,3,2,1,0:T(8,128)S(1)} %collective-permute-done.14) | copy-start | bytes 98308
  133.3 2.2 collective-permute-start.17
  133.3 5.3 %collective-permute-start.16 = (f32[1,6,4,8,128]{4,3,2,1,0:T(8,128)S(1)}, f32[1,6,4,8,128]{4,3,2,1,0:T(8,128)S(1)}, u32[]{:S(2)}, u32[]{:S(2)}) collective-permute-start(f32[1,6,4,8,128]{4,3,2,1,0:T(8,128)S(1)} %get-tuple-element.55), channel_id=1, source_target_pairs={{0,32},{32,64},{64,96},{96,128},{128,160},{160,192},{192,224},{224... | collective-permute-start | bytes 294920 | tf_op jit(solution)/shard_map/ppermute | solution.py:326
  135.5 3.1 %copy-start.12 = (f32[1,6,4,8,128]{4,3,2,1,0:T(8,128)}, f32[1,6,4,8,128]{4,3,2,1,0:T(8,128)S(1)}, u32[]{:S(2)}) copy-start(f32[1,6,4,8,128]{4,3,2,1,0:T(8,128)S(1)} %collective-permute-done.17) | copy-start | bytes 294916
  138.5 0.6 copy-start.13
  162.7 7.5 %collective-permute-start.19 = (f32[2,4,1,8,128]{4,3,2,1,0:T(8,128)S(1)}, f32[2,4,1,8,128]{4,3,2,1,0:T(8,128)S(1)}, u32[]{:S(2)}, u32[]{:S(2)}) collective-permute-start(f32[2,4,1,8,128]{4,3,2,1,0:T(8,128)S(1)} %get-tuple-element.90), channel_id=1, source_target_pairs={{1,0},{2,1},{3,2},{5,4},{6,5},{7,6},{9,8},{10,9},{11,10},{13,12},{... | collective-permute-start | bytes 98312 | tf_op jit(solution)/shard_map/ppermute | solution.py:326
  164.0 7.8 %collective-permute-start.18 = (f32[2,4,1,8,128]{4,3,2,1,0:T(8,128)S(1)}, f32[2,4,1,8,128]{4,3,2,1,0:T(8,128)S(1)}, u32[]{:S(2)}, u32[]{:S(2)}) collective-permute-start(f32[2,4,1,8,128]{4,3,2,1,0:T(8,128)S(1)} %get-tuple-element.91), channel_id=1, source_target_pairs={{0,1},{1,2},{2,3},{4,5},{5,6},{6,7},{8,9},{9,10},{10,11},{12,13},{... | collective-permute-start | bytes 98312 | tf_op jit(solution)/shard_map/ppermute | solution.py:326
  170.3 23.3 %copy-start = (f32[2,4,1,8,128]{4,3,2,1,0:T(8,128)}, f32[2,4,1,8,128]{4,3,2,1,0:T(8,128)S(1)}, u32[]{:S(2)}) copy-start(f32[2,4,1,8,128]{4,3,2,1,0:T(8,128)S(1)} %collective-permute-done.19) | copy-start | bytes 98308
  171.8 21.7 %copy-start.1 = (f32[2,4,1,8,128]{4,3,2,1,0:T(8,128)}, f32[2,4,1,8,128]{4,3,2,1,0:T(8,128)S(1)}, u32[]{:S(2)}) copy-start(f32[2,4,1,8,128]{4,3,2,1,0:T(8,128)S(1)} %collective-permute-done.18) | copy-start | bytes 98308
  172.6 13.2 %collective-permute-start.21 = (f32[2,1,4,8,128]{4,3,2,1,0:T(8,128)S(1)}, f32[2,1,4,8,128]{4,3,2,1,0:T(8,128)S(1)}, u32[]{:S(2)}, u32[]{:S(2)}) collective-permute-start(f32[2,1,4,8,128]{4,3,2,1,0:T(8,128)S(1)} %get-tuple-element.82), channel_id=1, source_target_pairs={{4,0},{8,4},{12,8},{16,12},{20,16},{24,20},{28,24},{5,1},{9,5},{13... | collective-permute-start | bytes 98312 | tf_op jit(solution)/shard_map/ppermute | solution.py:326
  174.5 12.8 %collective-permute-start.20 = (f32[2,1,4,8,128]{4,3,2,1,0:T(8,128)S(1)}, f32[2,1,4,8,128]{4,3,2,1,0:T(8,128)S(1)}, u32[]{:S(2)}, u32[]{:S(2)}) collective-permute-start(f32[2,1,4,8,128]{4,3,2,1,0:T(8,128)S(1)} %get-tuple-element.83), channel_id=1, source_target_pairs={{0,4},{4,8},{8,12},{12,16},{16,20},{20,24},{24,28},{1,5},{5,9},{9,... | collective-permute-start | bytes 98312 | tf_op jit(solution)/shard_map/ppermute | solution.py:326
  185.8 7.8 %copy-start.6 = (f32[2,1,4,8,128]{4,3,2,1,0:T(8,128)}, f32[2,1,4,8,128]{4,3,2,1,0:T(8,128)S(1)}, u32[]{:S(2)}) copy-start(f32[2,1,4,8,128]{4,3,2,1,0:T(8,128)S(1)} %collective-permute-done.21) | copy-start | bytes 98308
  187.3 6.2 %copy-start.7 = (f32[2,1,4,8,128]{4,3,2,1,0:T(8,128)}, f32[2,1,4,8,128]{4,3,2,1,0:T(8,128)S(1)}, u32[]{:S(2)}) copy-start(f32[2,1,4,8,128]{4,3,2,1,0:T(8,128)S(1)} %collective-permute-done.20) | copy-start | bytes 98308
  188.2 2.2 collective-permute-start.23
  188.2 5.3 %collective-permute-start.22 = (f32[1,6,4,8,128]{4,3,2,1,0:T(8,128)S(1)}, f32[1,6,4,8,128]{4,3,2,1,0:T(8,128)S(1)}, u32[]{:S(2)}, u32[]{:S(2)}) collective-permute-start(f32[1,6,4,8,128]{4,3,2,1,0:T(8,128)S(1)} %get-tuple-element.53), channel_id=1, source_target_pairs={{0,32},{32,64},{64,96},{96,128},{128,160},{160,192},{192,224},{224... | collective-permute-start | bytes 294920 | tf_op jit(solution)/shard_map/ppermute | solution.py:326
  190.4 3.1 %copy-start.14 = (f32[1,6,4,8,128]{4,3,2,1,0:T(8,128)}, f32[1,6,4,8,128]{4,3,2,1,0:T(8,128)S(1)}, u32[]{:S(2)}) copy-start(f32[1,6,4,8,128]{4,3,2,1,0:T(8,128)S(1)} %collective-permute-done.23) | copy-start | bytes 294916
  193.5 0.6 copy-start.15
  219.7 34.6 %all-to-all-start = ((f32[256,1,256]{2,1,0:T(1,128)}), f32[256,1,256]{2,1,0:T(1,128)S(1)}, u32[]{:S(2)}, u32[]{:S(2)}) async-start(f32[256,1,256]{2,1,0:T(1,128)} %broadcast_in_dim.2), calls=%async_computation | async-start | bytes 524288 | tf_op jit(solution)/shard_map/all_to_all | solution.py:419
